TPU v7x, 128 devices: a whole 4x4x4 slice. The times are simulated.
128 devices in a mesh: row: 16 (over z, x), col: 8 (over y, core).
Axes of the slice: x: 4, y: 4, z: 4, core: 2. Of those that a mesh axis runs over, the one named last changes fastest.
Arguments:
- residual: bfloat16 [512, 1024, 256], P(('row', 'col')), may hold values from -6 to 6
- interface_inverse: bfloat16 [512, 1024, 1024], P(('row', 'col'))
- modes: bfloat16 [512, 1024, 32], P(('row', 'col')), may hold values from -0.375 to 0.375
- coarse_map: int32 [16384], P(('row', 'col')), may hold values from 0 to 16383, each once
- coarse_inverse: bfloat16 [16384, 16384], P('row', 'col')
- neighbours: int32 [512, 2], P(('row', 'col')), may hold values from 0 to 511, as said below
- block_sizes: int32 [512, 2], P(('row', 'col')), may hold values from 128 to 256, as said below
- block_offsets: int32 [512, 2], P(('row', 'col')), may hold values from 0 to 384, as said below
Outputs:
- preconditioned: bfloat16 [512, 1024, 256], P(('row', 'col'))
Inputs may be any that keep to these rules, and one draw needn't show every extreme that they name: In round k the neighbour of subdomain s is (g XOR a_k) * 4 + (s mod 4) XOR b_k with g = s div 4, where a_k, b_k are the same for all subdomains, a_k is nonzero and a_0 differs from a_1; neighbours are mutual. `block_sizes`: each is 128 or 256, and equal for both sides of a shared block. `block_offsets`: the block of round k lies inside rows [k * 256, (k + 1) * 256) and starts at k * 256 or k * 256 + 256 // 2.
All inputs are finite; a program needn't handle non-finite values.
Results may differ from a plain program's by a relative error of at most 0.0052.
Values may be sent and summed in bfloat16 or wider, within the bound.
No kernel may reach another device: no remote copies, remote signals or barrier semaphores. Data moves between devices by JAX's collectives and lax.ppermute only.
A program may use at most 128 MiB of HBM per device.

v0:
```python
import jax
import jax.numpy as jnp
from jax import lax
from jax.sharding import PartitionSpec as P

MODES = 32
SHARE = 256


def from_partner(value, axis, apart):
    return lax.ppermute(value, axis, [(i, i ^ 1 << apart) for i in range(lax.axis_size(axis))])


def travel(carried, partner_bits):
    total_bits = lax.axis_size(("row", "col")).bit_length() - 1
    for level in range(total_bits):
        other = from_partner(carried, ("row", "col"), level)
        chosen = jnp.bitwise_and(jnp.right_shift(partner_bits, level), 1) == 1
        carried = jnp.where(chosen, other, carried)
    return carried


def neighbour_sum(field, neighbours, block_sizes, block_offsets):
    count = field.shape[0]
    cases = field.shape[2]
    trace_len = field.shape[1]
    half_share = SHARE // 2
    device_index = lax.axis_index(("row", "col"))
    row_index = jnp.arange(SHARE)
    summed = field.astype(jnp.float32)
    for which in range(2):
        start = which * SHARE
        region = field[:, start : start + SHARE]
        relative = block_offsets[:, which] - start
        shifted = jnp.concatenate(
            [region[:, half_share:], jnp.zeros((count, half_share, cases), jnp.bfloat16)], 1
        )
        aligned = jnp.where((relative == 0)[:, None, None], region, shifted)
        inside = (row_index[None, :] < block_sizes[:, which][:, None])[:, :, None]
        aligned = jnp.where(inside, aligned, jnp.zeros_like(aligned))
        partner_bits = jnp.bitwise_xor(neighbours[0, which] // count, device_index)
        received = travel(aligned, partner_bits)
        arrived = jnp.take(received, neighbours[:, which] % count, axis=0)
        moved = jnp.concatenate(
            [jnp.zeros((count, half_share, cases), jnp.bfloat16), arrived[:, : SHARE - half_share]],
            1,
        )
        placed = jnp.where((relative == 0)[:, None, None], arrived, moved)
        summed = summed + jnp.pad(
            placed.astype(jnp.float32), ((0, 0), (start, trace_len - start - SHARE), (0, 0))
        )
    return summed


def weights_of(block_sizes, block_offsets, trace_len):
    trace_rows = jnp.arange(trace_len)
    covered = jnp.zeros((block_sizes.shape[0], trace_len), jnp.float32)
    for which in range(2):
        lower = block_offsets[:, which][:, None]
        upper = lower + block_sizes[:, which][:, None]
        covered = covered + jnp.where(
            (trace_rows[None, :] >= lower) & (trace_rows[None, :] < upper), 1.0, 0.0
        ).astype(jnp.float32)
    return 1.0 / (1.0 + covered)


def shards(
    residual,
    interface_inverse,
    modes,
    coarse_map,
    coarse_inverse,
    neighbours,
    block_sizes,
    block_offsets,
):
    count = residual.shape[0]
    trace_len = residual.shape[1]
    cases = residual.shape[2]
    omega = weights_of(block_sizes, block_offsets, trace_len)
    weighted = (
        omega[:, :, None] * neighbour_sum(residual, neighbours, block_sizes, block_offsets)
    ).astype(jnp.bfloat16)
    local_part = jnp.einsum(
        "sij,sjr->sir", interface_inverse, weighted, preferred_element_type=jnp.float32
    )
    restricted = jnp.einsum(
        "swm,swr->smr", modes, weighted, preferred_element_type=jnp.float32
    ).astype(jnp.bfloat16)
    restricted = restricted.reshape(count * MODES, cases)
    all_rhs, all_map = (
        lax.all_gather(restricted, ("row", "col"), axis=0, tiled=True),
        lax.all_gather(coarse_map, ("row", "col"), axis=0, tiled=True),
    )
    coarse_rhs = jnp.zeros((all_map.shape[0], cases), jnp.bfloat16).at[all_map].set(all_rhs)
    columns = coarse_inverse.shape[1]
    column_part = lax.dynamic_slice_in_dim(coarse_rhs, lax.axis_index("col") * columns, columns, 0)
    partial_sum = jnp.dot(coarse_inverse, column_part, preferred_element_type=jnp.float32)
    own_rows = lax.psum_scatter(partial_sum, "col", scatter_dimension=0, tiled=True).astype(
        jnp.bfloat16
    )
    coarse_full = lax.all_gather(own_rows, ("row", "col"), axis=0, tiled=True)
    picked = jnp.take(coarse_full, coarse_map, axis=0).reshape(count, MODES, cases)
    prolonged = local_part + jnp.einsum(
        "swm,smr->swr", modes, picked, preferred_element_type=jnp.float32
    )
    corrected = (omega[:, :, None] * prolonged).astype(jnp.bfloat16)
    return neighbour_sum(corrected, neighbours, block_sizes, block_offsets).astype(jnp.bfloat16)


def solution(mesh):
    return jax.shard_map(
        shards,
        mesh=mesh,
        in_specs=(
            P(("row", "col"), None, None),
            P(("row", "col"), None, None),
            P(("row", "col"), None, None),
            P(("row", "col")),
            P("row", "col"),
            P(("row", "col"), None),
            P(("row", "col"), None),
            P(("row", "col"), None),
        ),
        out_specs=P(("row", "col"), None, None),
        check_vma=False,
    )
```

profile of v0, /device:TPU:0, one launch (start us, length us, event | category | flops | bytes accessed | tf_op | source)
XLA Modules:
  0.0 567.4 jit_solution(5247554139306587757)
XLA Ops:
  8.1 3.0 copy.17
  16.9 1.7 collective-permute-start.1
  22.8 9.1 %collective-permute-done.1 = bf16[4,256,256]{1,2,0:T(8,128)(2,1)} collective-permute-done((bf16[4,256,256]{1,2,0:T(8,128)(2,1)S(1)}, bf16[4,256,256]{1,2,0:T(8,128)(2,1)}, u32[]{:S(2)}, u32[]{:S(2)}) %collective-permute-start.1) | collective-permute-done | bytes 524320 | tf_op jit(solution)/shard_map/ppermute | solution.py:11
  31.9 1.9 broadcast_select_fusion.21
  33.8 3.3 collective-permute-start.2
  37.1 6.1 %collective-permute-done.8 = bf16[4,256,256]{1,2,0:T(8,128)(2,1)} collective-permute-done((bf16[4,256,256]{1,2,0:T(8,128)(2,1)S(1)}, bf16[4,256,256]{1,2,0:T(8,128)(2,1)}, u32[]{:S(2)}, u32[]{:S(2)}) %collective-permute-start.8) | collective-permute-done | bytes 524320 | tf_op jit(solution)/shard_map/ppermute | solution.py:11
  44.2 3.4 collective-permute-start.9
  47.6 9.2 %collective-permute-done.2 = bf16[4,256,256]{1,2,0:T(8,128)(2,1)S(1)} collective-permute-done((bf16[4,256,256]{1,2,0:T(8,128)(2,1)}, bf16[4,256,256]{1,2,0:T(8,128)(2,1)S(1)}, u32[]{:S(2)}, u32[]{:S(2)}) %collective-permute-start.2) | collective-permute-done | bytes 524320 | tf_op jit(solution)/shard_map/ppermute | solution.py:11
  56.8 1.9 broadcast_select_fusion.23
  58.7 1.5 collective-permute-start.3
  60.2 7.1 %collective-permute-done.9 = bf16[4,256,256]{1,2,0:T(8,128)(2,1)} collective-permute-done((bf16[4,256,256]{1,2,0:T(8,128)(2,1)S(1)}, bf16[4,256,256]{1,2,0:T(8,128)(2,1)}, u32[]{:S(2)}, u32[]{:S(2)}) %collective-permute-start.9) | collective-permute-done | bytes 524320 | tf_op jit(solution)/shard_map/ppermute | solution.py:11
  67.3 1.6 collective-permute-start.10
  68.9 4.1 collective-permute-done.3
  74.1 3.1 collective-permute-start.4
  77.2 7.0 %collective-permute-done.10 = bf16[4,256,256]{1,2,0:T(8,128)(2,1)} collective-permute-done((bf16[4,256,256]{1,2,0:T(8,128)(2,1)S(1)}, bf16[4,256,256]{1,2,0:T(8,128)(2,1)}, u32[]{:S(2)}, u32[]{:S(2)}) %collective-permute-start.10) | collective-permute-done | bytes 524320 | tf_op jit(solution)/shard_map/ppermute | solution.py:11
  85.4 3.1 collective-permute-start.11
  88.5 9.2 %collective-permute-done.4 = bf16[4,256,256]{1,2,0:T(8,128)(2,1)} collective-permute-done((bf16[4,256,256]{1,2,0:T(8,128)(2,1)S(1)}, bf16[4,256,256]{1,2,0:T(8,128)(2,1)}, u32[]{:S(2)}, u32[]{:S(2)}) %collective-permute-start.4) | collective-permute-done | bytes 524320 | tf_op jit(solution)/shard_map/ppermute | solution.py:11
  98.8 2.0 collective-permute-start.5
  100.8 6.2 %collective-permute-done.11 = bf16[4,256,256]{1,2,0:T(8,128)(2,1)S(1)} collective-permute-done((bf16[4,256,256]{1,2,0:T(8,128)(2,1)S(1)}, bf16[4,256,256]{1,2,0:T(8,128)(2,1)S(1)}, u32[]{:S(2)}, u32[]{:S(2)}) %collective-permute-start.11) | collective-permute-done | bytes 524320 | tf_op jit(solution)/shard_map/ppermute | solution.py:11
  107.1 2.0 collective-permute-start.12
  109.1 1.4 collective-permute-done.5
  110.6 3.8 collective-permute-start.6
  114.4 7.7 %collective-permute-done.12 = bf16[4,256,256]{1,2,0:T(8,128)(2,1)} collective-permute-done((bf16[4,256,256]{1,2,0:T(8,128)(2,1)S(1)}, bf16[4,256,256]{1,2,0:T(8,128)(2,1)}, u32[]{:S(2)}, u32[]{:S(2)}) %collective-permute-start.12) | collective-permute-done | bytes 524320 | tf_op jit(solution)/shard_map/ppermute | solution.py:11
  122.1 1.9 broadcast_select_fusion.15
  124.0 3.9 collective-permute-start.13
  127.9 8.9 %collective-permute-done.6 = bf16[4,256,256]{1,2,0:T(8,128)(2,1)} collective-permute-done((bf16[4,256,256]{1,2,0:T(8,128)(2,1)S(1)}, bf16[4,256,256]{1,2,0:T(8,128)(2,1)}, u32[]{:S(2)}, u32[]{:S(2)}) %collective-permute-start.6) | collective-permute-done | bytes 524320 | tf_op jit(solution)/shard_map/ppermute | solution.py:11
  136.9 1.9 broadcast_select_fusion.31
  138.8 1.6 gather_fusion.1
  141.6 4.9 collective-permute-done.13
  148.6 2.4 convolution_convert_fusion
  151.1 27.7 %all-gather = s32[128,1,128]{2,1,0:T(1,128)S(1)} all-gather(s32[1,1,128]{2,1,0:T(1,128)S(1)} %bitcast.41), channel_id=1, replica_groups=mesh['row'=16,'col'=8] {'row','col'}, dimensions={0}, use_global_device_ids=true | all-gather | bytes 66048 | tf_op jit(solution)/shard_map/all_gather | solution.py:93
  178.9 36.6 %all-gather.4.cloned.1.call-done = bf16[16384,256]{1,0:T(8,128)(2,1)} async-done(((bf16[128,256]{1,0:T(8,128)(2,1)}), bf16[16384,256]{1,0:T(8,128)(2,1)}) %all-gather.4.cloned.1.call-update) | async-done | bytes 8388624 | tf_op jit(solution)/shard_map/all_gather | solution.py:92
  215.5 74.2 %scatter_custom_fusion = bf16[16384,256]{1,0:T(8,128)(2,1)} fusion(s32[16384]{0:T(1024)S(1)} %compare_select_fusion, bf16[16384,256]{1,0:T(8,128)(2,1)} %all-gather.4.cloned.1.call-done, bf16[]{:T(256)} %constant.108.clone.1), kind=kCustom, calls=%fused_computation.8 | custom fusion | bytes 8389120 | tf_op jit(solution)/shard_map/scatter | solution.py:95
  289.7 4.8 convolution_bitcast_fusion
  294.8 29.3 %reduce-scatter.2.cloned.1.call-done = f32[128,256]{0,1:T(8,128)} async-done(((f32[1024,256]{0,1:T(8,128)}), f32[128,256]{0,1:T(8,128)}) %reduce-scatter.2.cloned.1.call-update) | async-done | bytes 131088 | tf_op jit(solution)/shard_map/reduce_scatter | solution.py:99
  324.1 1.5 convert_element_type.41
  325.8 7.7 %fusion.8 = f32[4,256,1024]{2,1,0:T(8,128)} fusion(bf16[4,1024,1024]{2,1,0:T(8,128)(2,1)} %param.11, bf16[4,1024,256]{1,2,0:T(8,128)(2,1)S(1)} %copy.17, bf16[4,256,256]{1,2,0:T(8,128)(2,1)S(1)} %pad_select_fusion.2, bf16[4,256,256]{1,2,0:T(8,128)(2,1)S(1)} %copy-done.4, f32[4,1024]{1,0:T(4,128)S(1)} %add_divide_fusion), kind=kOutput, calls=%fused_computation.59 | convolution fusion | flops 2154823680 | bytes 15745024 | tf_op jit(solution)/shard_map/sij,sjr->sir/dot_general | solution.py:84
  333.5 71.5 %all-gather.6.cloned.1.call-done = bf16[16384,256]{0,1:T(8,128)(2,1)} async-done(((bf16[128,256]{0,1:T(8,128)(2,1)}), bf16[16384,256]{0,1:T(8,128)(2,1)}) %all-gather.6.cloned.1.call-update) | async-done | bytes 8388624 | tf_op jit(solution)/shard_map/all_gather | solution.py:102
  405.0 11.9 %copy.23 = bf16[16384,256]{1,0:T(8,128)(2,1)} copy(bf16[16384,256]{0,1:T(8,128)(2,1)} %all-gather.6.cloned.1.call-done) | data formatting | bytes 16777216 | tf_op jit(solution)/shard_map/all_gather | solution.py:102
  417.0 5.2 gather_fusion
  422.2 3.0 fusion.2
  426.5 1.4 collective-permute-done.14
  427.9 1.6 collective-permute-start.15
  430.2 12.5 %collective-permute-done.15 = bf16[4,256,256]{1,2,0:T(8,128)(2,1)S(1)} collective-permute-done((bf16[4,256,256]{1,2,0:T(8,128)(2,1)S(1)}, bf16[4,256,256]{1,2,0:T(8,128)(2,1)S(1)}, u32[]{:S(2)}, u32[]{:S(2)}) %collective-permute-start.15) | collective-permute-done | bytes 524320 | tf_op jit(solution)/shard_map/ppermute | solution.py:11
  442.8 3.1 collective-permute-start.16
  445.9 8.1 %collective-permute-done.22 = bf16[4,256,256]{1,2,0:T(8,128)(2,1)S(1)} collective-permute-done((bf16[4,256,256]{1,2,0:T(8,128)(2,1)S(1)}, bf16[4,256,256]{1,2,0:T(8,128)(2,1)S(1)}, u32[]{:S(2)}, u32[]{:S(2)}) %collective-permute-start.22) | collective-permute-done | bytes 524320 | tf_op jit(solution)/shard_map/ppermute | solution.py:11
  454.0 3.1 collective-permute-start.23
  457.1 10.3 %collective-permute-done.16 = bf16[4,256,256]{1,2,0:T(8,128)(2,1)S(1)} collective-permute-done((bf16[4,256,256]{1,2,0:T(8,128)(2,1)S(1)}, bf16[4,256,256]{1,2,0:T(8,128)(2,1)S(1)}, u32[]{:S(2)}, u32[]{:S(2)}) %collective-permute-start.16) | collective-permute-done | bytes 524320 | tf_op jit(solution)/shard_map/ppermute | solution.py:11
  467.5 1.3 collective-permute-start.17
  468.7 9.3 %collective-permute-done.23 = bf16[4,256,256]{1,2,0:T(8,128)(2,1)S(1)} collective-permute-done((bf16[4,256,256]{1,2,0:T(8,128)(2,1)S(1)}, bf16[4,256,256]{1,2,0:T(8,128)(2,1)S(1)}, u32[]{:S(2)}, u32[]{:S(2)}) %collective-permute-start.23) | collective-permute-done | bytes 524320 | tf_op jit(solution)/shard_map/ppermute | solution.py:11
  480.2 1.8 collective-permute-start.18
  482.1 10.9 %collective-permute-done.24 = bf16[4,256,256]{1,2,0:T(8,128)(2,1)S(1)} collective-permute-done((bf16[4,256,256]{1,2,0:T(8,128)(2,1)S(1)}, bf16[4,256,256]{1,2,0:T(8,128)(2,1)S(1)}, u32[]{:S(2)}, u32[]{:S(2)}) %collective-permute-start.24) | collective-permute-done | bytes 524320 | tf_op jit(solution)/shard_map/ppermute | solution.py:11
  493.0 1.8 collective-permute-start.25
  494.9 10.8 %collective-permute-done.18 = bf16[4,256,256]{1,2,0:T(8,128)(2,1)S(1)} collective-permute-done((bf16[4,256,256]{1,2,0:T(8,128)(2,1)S(1)}, bf16[4,256,256]{1,2,0:T(8,128)(2,1)S(1)}, u32[]{:S(2)}, u32[]{:S(2)}) %collective-permute-start.18) | collective-permute-done | bytes 524320 | tf_op jit(solution)/shard_map/ppermute | solution.py:11
  506.3 9.0 %collective-permute-done.25 = bf16[4,256,256]{1,2,0:T(8,128)(2,1)S(1)} collective-permute-done((bf16[4,256,256]{1,2,0:T(8,128)(2,1)S(1)}, bf16[4,256,256]{1,2,0:T(8,128)(2,1)S(1)}, u32[]{:S(2)}, u32[]{:S(2)}) %collective-permute-start.25) | collective-permute-done | bytes 524320 | tf_op jit(solution)/shard_map/ppermute | solution.py:11
  516.7 2.2 collective-permute-start.20
  518.9 11.4 %collective-permute-done.26 = bf16[4,256,256]{1,2,0:T(8,128)(2,1)S(1)} collective-permute-done((bf16[4,256,256]{1,2,0:T(8,128)(2,1)S(1)}, bf16[4,256,256]{1,2,0:T(8,128)(2,1)S(1)}, u32[]{:S(2)}, u32[]{:S(2)}) %collective-permute-start.26) | collective-permute-done | bytes 524320 | tf_op jit(solution)/shard_map/ppermute | solution.py:11
  531.2 2.2 collective-permute-start.27
  533.3 9.1 %collective-permute-done.20 = bf16[4,256,256]{1,2,0:T(8,128)(2,1)S(1)} collective-permute-done((bf16[4,256,256]{1,2,0:T(8,128)(2,1)S(1)}, bf16[4,256,256]{1,2,0:T(8,128)(2,1)S(1)}, u32[]{:S(2)}, u32[]{:S(2)}) %collective-permute-start.20) | collective-permute-done | bytes 524320 | tf_op jit(solution)/shard_map/ppermute | solution.py:11
  543.5 7.8 %collective-permute-done.27 = bf16[4,256,256]{1,2,0:T(8,128)(2,1)} collective-permute-done((bf16[4,256,256]{1,2,0:T(8,128)(2,1)}, bf16[4,256,256]{1,2,0:T(8,128)(2,1)}, u32[]{:S(2)}, u32[]{:S(2)}) %collective-permute-start.27) | collective-permute-done | bytes 524320 | tf_op jit(solution)/shard_map/ppermute | solution.py:11
  551.3 1.9 broadcast_select_fusion.16
  553.2 1.6 gather_fusion.4
  555.2 1.8 add_convert_fusion
  557.0 3.9 copy.24
  (88 shorter events, 23.3 us)
Async XLA Ops:
  6.5 142.1 %copy-start = (bf16[4,1024,32]{1,2,0:T(8,128)(2,1)S(1)}, bf16[4,1024,32]{1,2,0:T(8,128)(2,1)}, u32[]{:S(2)}) copy-start(bf16[4,1024,32]{1,2,0:T(8,128)(2,1)} %param.12) | copy-start | bytes 786436
  6.5 5.9 %copy-start.5 = (s32[4,2]{0,1:T(2,128)S(1)}, s32[4,2]{0,1:T(2,128)}, u32[]{:S(2)}) copy-start(s32[4,2]{0,1:T(2,128)} %param.15) | copy-start | bytes 100
  6.5 208.9 %all-gather.4.cloned.1.call-start = ((), (), s32[]{:S(2)}) async-start(), calls=%async_computation.1 | async-start | bytes 8454144 | tf_op jit(solution)/shard_map/all_gather | solution.py:92
  11.8 4.0 copy-start.3
  11.8 9.4 %copy-start.2 = (bf16[4,256,256]{1,2,0:T(8,128)(2,1)}, bf16[4,256,256]{1,2,0:T(8,128)(2,1)S(1)}, u32[]{:S(2)}) copy-start(bf16[4,256,256]{1,2,0:T(8,128)(2,1)S(1)} %get-tuple-element.15) | copy-start | bytes 1572868
  11.8 4.0 collective-permute-start
  11.9 9.3 %collective-permute-start.7 = (bf16[4,256,256]{1,2,0:T(8,128)(2,1)S(1)}, bf16[4,256,256]{1,2,0:T(8,128)(2,1)}, u32[]{:S(2)}, u32[]{:S(2)}) collective-permute-start(bf16[4,256,256]{1,2,0:T(8,128)(2,1)S(1)} %get-tuple-element.15), channel_id=1, source_target_pairs={{0,1},{1,0},{2,3},{3,2},{4,5},{5,4},{6,7},{7,6},{8,9},{9,8},{10,11... | collective-permute-start | bytes 1572872 | tf_op jit(solution)/shard_map/ppermute | solution.py:11
  16.9 15.0 %collective-permute-start.1 = (bf16[4,256,256]{1,2,0:T(8,128)(2,1)S(1)}, bf16[4,256,256]{1,2,0:T(8,128)(2,1)}, u32[]{:S(2)}, u32[]{:S(2)}) collective-permute-start(bf16[4,256,256]{1,2,0:T(8,128)(2,1)S(1)} %broadcast_select_fusion.19), channel_id=1, source_target_pairs={{0,2},{1,3},{2,0},{3,1},{4,6},{5,7},{6,4},{7,5},{8,10},{9,11},{10,... | collective-permute-start | bytes 1572872 | tf_op jit(solution)/shard_map/ppermute | solution.py:11
  22.3 14.7 %copy-start.1 = (bf16[4,256,256]{1,2,0:T(8,128)(2,1)}, bf16[4,256,256]{1,2,0:T(8,128)(2,1)S(1)}, u32[]{:S(2)}) copy-start(bf16[4,256,256]{1,2,0:T(8,128)(2,1)S(1)} %broadcast_select_fusion.5) | copy-start | bytes 1572868
  22.3 20.8 %collective-permute-start.8 = (bf16[4,256,256]{1,2,0:T(8,128)(2,1)S(1)}, bf16[4,256,256]{1,2,0:T(8,128)(2,1)}, u32[]{:S(2)}, u32[]{:S(2)}) collective-permute-start(bf16[4,256,256]{1,2,0:T(8,128)(2,1)S(1)} %broadcast_select_fusion.5), channel_id=1, source_target_pairs={{0,2},{1,3},{2,0},{3,1},{4,6},{5,7},{6,4},{7,5},{8,10},{9,11},{10,... | collective-permute-start | bytes 1572872 | tf_op jit(solution)/shard_map/ppermute | solution.py:11
  33.8 23.0 %collective-permute-start.2 = (bf16[4,256,256]{1,2,0:T(8,128)(2,1)}, bf16[4,256,256]{1,2,0:T(8,128)(2,1)S(1)}, u32[]{:S(2)}, u32[]{:S(2)}) collective-permute-start(bf16[4,256,256]{1,2,0:T(8,128)(2,1)} %broadcast_select_fusion.21), channel_id=1, source_target_pairs={{0,4},{1,5},{2,6},{3,7},{4,0},{5,1},{6,2},{7,3},{8,12},{9,13},{10,... | collective-permute-start | bytes 1572872 | tf_op jit(solution)/shard_map/ppermute | solution.py:11
  44.2 23.0 %collective-permute-start.9 = (bf16[4,256,256]{1,2,0:T(8,128)(2,1)S(1)}, bf16[4,256,256]{1,2,0:T(8,128)(2,1)}, u32[]{:S(2)}, u32[]{:S(2)}) collective-permute-start(bf16[4,256,256]{1,2,0:T(8,128)(2,1)S(1)} %broadcast_select_fusion.7), channel_id=1, source_target_pairs={{0,4},{1,5},{2,6},{3,7},{4,0},{5,1},{6,2},{7,3},{8,12},{9,13},{10,... | collective-permute-start | bytes 1572872 | tf_op jit(solution)/shard_map/ppermute | solution.py:11
  58.7 14.3 %collective-permute-start.3 = (bf16[4,256,256]{1,2,0:T(8,128)(2,1)}, bf16[4,256,256]{1,2,0:T(8,128)(2,1)}, u32[]{:S(2)}, u32[]{:S(2)}) collective-permute-start(bf16[4,256,256]{1,2,0:T(8,128)(2,1)} %broadcast_select_fusion.23), channel_id=1, source_target_pairs={{0,8},{1,9},{2,10},{3,11},{4,12},{5,13},{6,14},{7,15},{8,0},{9,1},... | collective-permute-start | bytes 1572872 | tf_op jit(solution)/shard_map/ppermute | solution.py:11
  67.3 16.9 %collective-permute-start.10 = (bf16[4,256,256]{1,2,0:T(8,128)(2,1)S(1)}, bf16[4,256,256]{1,2,0:T(8,128)(2,1)}, u32[]{:S(2)}, u32[]{:S(2)}) collective-permute-start(bf16[4,256,256]{1,2,0:T(8,128)(2,1)S(1)} %broadcast_select_fusion.9), channel_id=1, source_target_pairs={{0,8},{1,9},{2,10},{3,11},{4,12},{5,13},{6,14},{7,15},{8,0},{9,1},... | collective-permute-start | bytes 1572872 | tf_op jit(solution)/shard_map/ppermute | solution.py:11
  74.1 23.6 %collective-permute-start.4 = (bf16[4,256,256]{1,2,0:T(8,128)(2,1)S(1)}, bf16[4,256,256]{1,2,0:T(8,128)(2,1)}, u32[]{:S(2)}, u32[]{:S(2)}) collective-permute-start(bf16[4,256,256]{1,2,0:T(8,128)(2,1)S(1)} %broadcast_select_fusion.25), channel_id=1, source_target_pairs={{0,16},{1,17},{2,18},{3,19},{4,20},{5,21},{6,22},{7,23},{8,24},{9,... | collective-permute-start | bytes 1572872 | tf_op jit(solution)/shard_map/ppermute | solution.py:11
  85.4 21.7 %collective-permute-start.11 = (bf16[4,256,256]{1,2,0:T(8,128)(2,1)S(1)}, bf16[4,256,256]{1,2,0:T(8,128)(2,1)S(1)}, u32[]{:S(2)}, u32[]{:S(2)}) collective-permute-start(bf16[4,256,256]{1,2,0:T(8,128)(2,1)S(1)} %broadcast_select_fusion.11), channel_id=1, source_target_pairs={{0,16},{1,17},{2,18},{3,19},{4,20},{5,21},{6,22},{7,23},{8,24},{9,... | collective-permute-start | bytes 1572872 | tf_op jit(solution)/shard_map/ppermute | solution.py:11
  98.8 11.7 %collective-permute-start.5 = (bf16[4,256,256]{1,2,0:T(8,128)(2,1)S(1)}, bf16[4,256,256]{1,2,0:T(8,128)(2,1)S(1)}, u32[]{:S(2)}, u32[]{:S(2)}) collective-permute-start(bf16[4,256,256]{1,2,0:T(8,128)(2,1)S(1)} %broadcast_select_fusion.27), channel_id=1, source_target_pairs={{0,32},{1,33},{2,34},{3,35},{4,36},{5,37},{6,38},{7,39},{8,40},{9,... | collective-permute-start | bytes 1572872 | tf_op jit(solution)/shard_map/ppermute | solution.py:11
  107.1 15.0 %collective-permute-start.12 = (bf16[4,256,256]{1,2,0:T(8,128)(2,1)S(1)}, bf16[4,256,256]{1,2,0:T(8,128)(2,1)}, u32[]{:S(2)}, u32[]{:S(2)}) collective-permute-start(bf16[4,256,256]{1,2,0:T(8,128)(2,1)S(1)} %broadcast_select_fusion.13), channel_id=1, source_target_pairs={{0,32},{1,33},{2,34},{3,35},{4,36},{5,37},{6,38},{7,39},{8,40},{9,... | collective-permute-start | bytes 1572872 | tf_op jit(solution)/shard_map/ppermute | solution.py:11
  110.6 26.3 %collective-permute-start.6 = (bf16[4,256,256]{1,2,0:T(8,128)(2,1)S(1)}, bf16[4,256,256]{1,2,0:T(8,128)(2,1)}, u32[]{:S(2)}, u32[]{:S(2)}) collective-permute-start(bf16[4,256,256]{1,2,0:T(8,128)(2,1)S(1)} %broadcast_select_fusion.29), channel_id=1, source_target_pairs={{0,64},{1,65},{2,66},{3,67},{4,68},{5,69},{6,70},{7,71},{8,72},{9,... | collective-permute-start | bytes 1572872 | tf_op jit(solution)/shard_map/ppermute | solution.py:11
  124.0 22.5 %collective-permute-start.13 = (bf16[4,256,256]{1,2,0:T(8,128)(2,1)}, bf16[4,256,256]{1,2,0:T(8,128)(2,1)}, u32[]{:S(2)}, u32[]{:S(2)}) collective-permute-start(bf16[4,256,256]{1,2,0:T(8,128)(2,1)} %broadcast_select_fusion.15), channel_id=1, source_target_pairs={{0,64},{1,65},{2,66},{3,67},{4,68},{5,69},{6,70},{7,71},{8,72},{9,... | collective-permute-start | bytes 1572872 | tf_op jit(solution)/shard_map/ppermute | solution.py:11
  148.4 2.7 copy-start.6
  151.1 173.0 %reduce-scatter.2.cloned.1.call-start = ((), (), s32[]{:S(2)}) async-start(), calls=%async_computation.2 | async-start | bytes 1179648 | tf_op jit(solution)/shard_map/reduce_scatter | solution.py:99
  289.7 36.1 %copy-start.4 = (bf16[4,256,256]{1,2,0:T(8,128)(2,1)S(1)}, bf16[4,256,256]{1,2,0:T(8,128)(2,1)}, u32[]{:S(2)}) copy-start(bf16[4,256,256]{1,2,0:T(8,128)(2,1)} %pad_select_fusion.3) | copy-start | bytes 1572868
  294.5 110.5 %all-gather.6.cloned.1.call-start = ((), (), s32[]{:S(2)}) async-start(), calls=%async_computation.3 | async-start | bytes 8454144 | tf_op jit(solution)/shard_map/all_gather | solution.py:102
  425.9 2.0 collective-permute-start.14
  426.2 3.3 collective-permute-start.21
  427.9 14.8 %collective-permute-start.15 = (bf16[4,256,256]{1,2,0:T(8,128)(2,1)S(1)}, bf16[4,256,256]{1,2,0:T(8,128)(2,1)S(1)}, u32[]{:S(2)}, u32[]{:S(2)}) collective-permute-start(bf16[4,256,256]{1,2,0:T(8,128)(2,1)S(1)} %broadcast_select_fusion.18), channel_id=1, source_target_pairs={{0,2},{1,3},{2,0},{3,1},{4,6},{5,7},{6,4},{7,5},{8,10},{9,11},{10,... | collective-permute-start | bytes 1572872 | tf_op jit(solution)/shard_map/ppermute | solution.py:11
  429.6 24.4 %collective-permute-start.22 = (bf16[4,256,256]{1,2,0:T(8,128)(2,1)S(1)}, bf16[4,256,256]{1,2,0:T(8,128)(2,1)S(1)}, u32[]{:S(2)}, u32[]{:S(2)}) collective-permute-start(bf16[4,256,256]{1,2,0:T(8,128)(2,1)S(1)} %broadcast_select_fusion.4), channel_id=1, source_target_pairs={{0,2},{1,3},{2,0},{3,1},{4,6},{5,7},{6,4},{7,5},{8,10},{9,11},{10,... | collective-permute-start | bytes 1572872 | tf_op jit(solution)/shard_map/ppermute | solution.py:11
  442.8 24.6 %collective-permute-start.16 = (bf16[4,256,256]{1,2,0:T(8,128)(2,1)S(1)}, bf16[4,256,256]{1,2,0:T(8,128)(2,1)S(1)}, u32[]{:S(2)}, u32[]{:S(2)}) collective-permute-start(bf16[4,256,256]{1,2,0:T(8,128)(2,1)S(1)} %broadcast_select_fusion.20), channel_id=1, source_target_pairs={{0,4},{1,5},{2,6},{3,7},{4,0},{5,1},{6,2},{7,3},{8,12},{9,13},{10,... | collective-permute-start | bytes 1572872 | tf_op jit(solution)/shard_map/ppermute | solution.py:11
  454.0 23.9 %collective-permute-start.23 = (bf16[4,256,256]{1,2,0:T(8,128)(2,1)S(1)}, bf16[4,256,256]{1,2,0:T(8,128)(2,1)S(1)}, u32[]{:S(2)}, u32[]{:S(2)}) collective-permute-start(bf16[4,256,256]{1,2,0:T(8,128)(2,1)S(1)} %broadcast_select_fusion.6), channel_id=1, source_target_pairs={{0,4},{1,5},{2,6},{3,7},{4,0},{5,1},{6,2},{7,3},{8,12},{9,13},{10,... | collective-permute-start | bytes 1572872 | tf_op jit(solution)/shard_map/ppermute | solution.py:11
  467.5 12.7 %collective-permute-start.17 = (bf16[4,256,256]{1,2,0:T(8,128)(2,1)S(1)}, bf16[4,256,256]{1,2,0:T(8,128)(2,1)S(1)}, u32[]{:S(2)}, u32[]{:S(2)}) collective-permute-start(bf16[4,256,256]{1,2,0:T(8,128)(2,1)S(1)} %broadcast_select_fusion.22), channel_id=1, source_target_pairs={{0,8},{1,9},{2,10},{3,11},{4,12},{5,13},{6,14},{7,15},{8,0},{9,1},... | collective-permute-start | bytes 1572872 | tf_op jit(solution)/shard_map/ppermute | solution.py:11
  478.0 14.9 %collective-permute-start.24 = (bf16[4,256,256]{1,2,0:T(8,128)(2,1)S(1)}, bf16[4,256,256]{1,2,0:T(8,128)(2,1)S(1)}, u32[]{:S(2)}, u32[]{:S(2)}) collective-permute-start(bf16[4,256,256]{1,2,0:T(8,128)(2,1)S(1)} %broadcast_select_fusion.8), channel_id=1, source_target_pairs={{0,8},{1,9},{2,10},{3,11},{4,12},{5,13},{6,14},{7,15},{8,0},{9,1},... | collective-permute-start | bytes 1572872 | tf_op jit(solution)/shard_map/ppermute | solution.py:11
  480.2 25.5 %collective-permute-start.18 = (bf16[4,256,256]{1,2,0:T(8,128)(2,1)S(1)}, bf16[4,256,256]{1,2,0:T(8,128)(2,1)S(1)}, u32[]{:S(2)}, u32[]{:S(2)}) collective-permute-start(bf16[4,256,256]{1,2,0:T(8,128)(2,1)S(1)} %broadcast_select_fusion.24), channel_id=1, source_target_pairs={{0,16},{1,17},{2,18},{3,19},{4,20},{5,21},{6,22},{7,23},{8,24},{9,... | collective-permute-start | bytes 1572872 | tf_op jit(solution)/shard_map/ppermute | solution.py:11
  493.0 22.3 %collective-permute-start.25 = (bf16[4,256,256]{1,2,0:T(8,128)(2,1)S(1)}, bf16[4,256,256]{1,2,0:T(8,128)(2,1)S(1)}, u32[]{:S(2)}, u32[]{:S(2)}) collective-permute-start(bf16[4,256,256]{1,2,0:T(8,128)(2,1)S(1)} %broadcast_select_fusion.10), channel_id=1, source_target_pairs={{0,16},{1,17},{2,18},{3,19},{4,20},{5,21},{6,22},{7,23},{8,24},{9,... | collective-permute-start | bytes 1572872 | tf_op jit(solution)/shard_map/ppermute | solution.py:11
  505.7 10.8 %collective-permute-start.19 = (bf16[4,256,256]{1,2,0:T(8,128)(2,1)S(1)}, bf16[4,256,256]{1,2,0:T(8,128)(2,1)S(1)}, u32[]{:S(2)}, u32[]{:S(2)}) collective-permute-start(bf16[4,256,256]{1,2,0:T(8,128)(2,1)S(1)} %broadcast_select_fusion.26), channel_id=1, source_target_pairs={{0,32},{1,33},{2,34},{3,35},{4,36},{5,37},{6,38},{7,39},{8,40},{9,... | collective-permute-start | bytes 1572872 | tf_op jit(solution)/shard_map/ppermute | solution.py:11
  515.4 14.9 %collective-permute-start.26 = (bf16[4,256,256]{1,2,0:T(8,128)(2,1)S(1)}, bf16[4,256,256]{1,2,0:T(8,128)(2,1)S(1)}, u32[]{:S(2)}, u32[]{:S(2)}) collective-permute-start(bf16[4,256,256]{1,2,0:T(8,128)(2,1)S(1)} %broadcast_select_fusion.12), channel_id=1, source_target_pairs={{0,32},{1,33},{2,34},{3,35},{4,36},{5,37},{6,38},{7,39},{8,40},{9,... | collective-permute-start | bytes 1572872 | tf_op jit(solution)/shard_map/ppermute | solution.py:11
  516.7 25.8 %collective-permute-start.20 = (bf16[4,256,256]{1,2,0:T(8,128)(2,1)S(1)}, bf16[4,256,256]{1,2,0:T(8,128)(2,1)S(1)}, u32[]{:S(2)}, u32[]{:S(2)}) collective-permute-start(bf16[4,256,256]{1,2,0:T(8,128)(2,1)S(1)} %broadcast_select_fusion.28), channel_id=1, source_target_pairs={{0,64},{1,65},{2,66},{3,67},{4,68},{5,69},{6,70},{7,71},{8,72},{9,... | collective-permute-start | bytes 1572872 | tf_op jit(solution)/shard_map/ppermute | solution.py:11
  531.2 20.1 %collective-permute-start.27 = (bf16[4,256,256]{1,2,0:T(8,128)(2,1)}, bf16[4,256,256]{1,2,0:T(8,128)(2,1)}, u32[]{:S(2)}, u32[]{:S(2)}) collective-permute-start(bf16[4,256,256]{1,2,0:T(8,128)(2,1)} %broadcast_select_fusion.14), channel_id=1, source_target_pairs={{0,64},{1,65},{2,66},{3,67},{4,68},{5,69},{6,70},{7,71},{8,72},{9,... | collective-permute-start | bytes 1572872 | tf_op jit(solution)/shard_map/ppermute | solution.py:11
Sparse Core Ops, SparseCore 0:
  151.2 64.2 all-gather.3
  294.7 29.3 reduce-scatter.1
  326.9 78.0 all-gather.5
where the time goes:
time: 569 us; the launch traced here: 567 us
  waiting for transfers between devices  321 us (56%)
  local copies, waits for them, and re-layouts  104 us (18%)
  starting transfers between devices  51.4 us (9%)
  blocking collectives  27.7 us (5%)
  other arithmetic  27.3 us (5%)
  between operations  18.8 us (3%)
  matrix products  18 us (3%)
    ppermute x28, waiting for transfers between devices, from_partner(): lax.ppermute(value, axis, [(i, i ^ 1 << apart) for i in range(lax.axis_si...  183 us
    scatter x1, local copies, waits for them, and re-layouts, shards(): jnp.zeros((all_map.shape[0], cases), jnp.bfloat16).at[all_map].set(all_rhs)  74.2 us
    all_gather x1, waiting for transfers between devices, shards(): coarse_full = lax.all_gather(own_rows, ('row', 'col'), axis=0, tiled=True)  71.5 us
    ppermute x28, starting transfers between devices, from_partner(): lax.ppermute(value, axis, [(i, i ^ 1 << apart) for i in range(lax.axis_si...  51.1 us
    all_gather x1, waiting for transfers between devices, shards(): lax.all_gather(restricted, ('row', 'col'), axis=0, tiled=True)  36.6 us
    reduce_scatter x1, waiting for transfers between devices, shards(): lax.psum_scatter(partial_sum, 'col', scatter_dimension=0, tiled=True)  29.3 us
    all_gather x1, blocking collectives, shards(): lax.all_gather(coarse_map, ('row', 'col'), axis=0, tiled=True)  27.7 us
    select_n x28, other arithmetic, travel(): carried = jnp.where(chosen, other, carried)  18.9 us
  transfers between devices with their start and end apart: 31, of which 28 were waited for; matrix products, arithmetic and copies ran while one was open for 5% of the time, Pallas kernels for 0%

commit v1 on v0

--- a/solution.py
+++ b/solution.py
@@ -89,7 +89,12 @@
     ).astype(jnp.bfloat16)
     restricted = restricted.reshape(count * MODES, cases)
     all_rhs, all_map = (
-        lax.all_gather(restricted, ("row", "col"), axis=0, tiled=True),
+        jnp.concatenate(
+            lax.all_to_all(
+                jnp.stack([restricted] * lax.axis_size(("row", "col"))), ("row", "col"), 0, 0
+            ),
+            axis=0,
+        ),
         lax.all_gather(coarse_map, ("row", "col"), axis=0, tiled=True),
     )
     coarse_rhs = jnp.zeros((all_map.shape[0], cases), jnp.bfloat16).at[all_map].set(all_rhs)

time: 569 us -> 635 us (1.12)
  blocking collectives: 27.7 us -> 121 us
  waiting for transfers between devices: 321 us -> 284 us
    all_gather x1, blocking collectives: 27.7 us -> 121 us  [shards(): lax.all_gather(coarse_map, ('row', 'col'), axis=0, tiled=True)]
    all_gather x1 -> x0, waiting for transfers between devices: 36.6 us -> none  [shards(): lax.all_gather(restricted, ('row', 'col'), axis=0, tiled=True)]
  transfers between devices with their start and end apart: 31 -> 31, of which waited for: 28 -> 27; matrix products, arithmetic and copies ran while one was open for 5% -> 4% of each run, Pallas kernels for 0% -> 0%
where the time goes in v1:
time: 635 us; the launch traced here: 634 us
  waiting for transfers between devices  284 us (45%)
  blocking collectives  121 us (19%)
  local copies, waits for them, and re-layouts  108 us (17%)
  starting transfers between devices  57.5 us (9%)
  other arithmetic  27.3 us (4%)
  between operations  18.6 us (3%)
  matrix products  17.3 us (3%)
    ppermute x28, waiting for transfers between devices, from_partner(): lax.ppermute(value, axis, [(i, i ^ 1 << apart) for i in range(lax.axis_si...  183 us
    all_gather x1, blocking collectives, shards(): lax.all_gather(coarse_map, ('row', 'col'), axis=0, tiled=True)  121 us
    scatter x1, local copies, waits for them, and re-layouts, shards(): jnp.zeros((all_map.shape[0], cases), jnp.bfloat16).at[all_map].set(all_rhs)  74.2 us
    all_gather x1, waiting for transfers between devices, shards(): coarse_full = lax.all_gather(own_rows, ('row', 'col'), axis=0, tiled=True)  71.4 us
    ppermute x28, starting transfers between devices, from_partner(): lax.ppermute(value, axis, [(i, i ^ 1 << apart) for i in range(lax.axis_si...  51.1 us
    reduce_scatter x1, waiting for transfers between devices, shards(): lax.psum_scatter(partial_sum, 'col', scatter_dimension=0, tiled=True)  29.6 us
    select_n x28, other arithmetic, travel(): carried = jnp.where(chosen, other, carried)  18.9 us
  transfers between devices with their start and end apart: 31, of which 27 were waited for; matrix products, arithmetic and copies ran while one was open for 4% of the time, Pallas kernels for 0%

profile of v1, /device:TPU:0, one launch (start us, length us, event | category | flops | bytes accessed | tf_op | source)
XLA Modules:
  0.0 633.9 jit_solution(2983704863314774877)
XLA Ops:
  8.1 3.0 copy.17
  16.6 1.7 collective-permute-start.1
  22.2 9.4 %collective-permute-done.1 = bf16[4,256,256]{1,2,0:T(8,128)(2,1)} collective-permute-done((bf16[4,256,256]{1,2,0:T(8,128)(2,1)S(1)}, bf16[4,256,256]{1,2,0:T(8,128)(2,1)}, u32[]{:S(2)}, u32[]{:S(2)}) %collective-permute-start.1) | collective-permute-done | bytes 524320 | tf_op jit(solution)/shard_map/ppermute | solution.py:11
  31.6 1.9 broadcast_select_fusion.21
  33.5 3.3 collective-permute-start.2
  36.8 6.1 collective-permute-done.8
  43.9 3.4 collective-permute-start.9
  47.3 9.2 %collective-permute-done.2 = bf16[4,256,256]{1,2,0:T(8,128)(2,1)S(1)} collective-permute-done((bf16[4,256,256]{1,2,0:T(8,128)(2,1)}, bf16[4,256,256]{1,2,0:T(8,128)(2,1)S(1)}, u32[]{:S(2)}, u32[]{:S(2)}) %collective-permute-start.2) | collective-permute-done | bytes 524320 | tf_op jit(solution)/shard_map/ppermute | solution.py:11
  56.5 1.9 broadcast_select_fusion.23
  58.4 1.5 collective-permute-start.3
  59.9 7.1 %collective-permute-done.9 = bf16[4,256,256]{1,2,0:T(8,128)(2,1)} collective-permute-done((bf16[4,256,256]{1,2,0:T(8,128)(2,1)S(1)}, bf16[4,256,256]{1,2,0:T(8,128)(2,1)}, u32[]{:S(2)}, u32[]{:S(2)}) %collective-permute-start.9) | collective-permute-done | bytes 524320 | tf_op jit(solution)/shard_map/ppermute | solution.py:11
  67.0 1.6 collective-permute-start.10
  68.6 4.1 collective-permute-done.3
  73.8 3.1 collective-permute-start.4
  76.9 7.0 %collective-permute-done.10 = bf16[4,256,256]{1,2,0:T(8,128)(2,1)} collective-permute-done((bf16[4,256,256]{1,2,0:T(8,128)(2,1)S(1)}, bf16[4,256,256]{1,2,0:T(8,128)(2,1)}, u32[]{:S(2)}, u32[]{:S(2)}) %collective-permute-start.10) | collective-permute-done | bytes 524320 | tf_op jit(solution)/shard_map/ppermute | solution.py:11
  85.0 3.1 collective-permute-start.11
  88.1 9.2 %collective-permute-done.4 = bf16[4,256,256]{1,2,0:T(8,128)(2,1)} collective-permute-done((bf16[4,256,256]{1,2,0:T(8,128)(2,1)S(1)}, bf16[4,256,256]{1,2,0:T(8,128)(2,1)}, u32[]{:S(2)}, u32[]{:S(2)}) %collective-permute-start.4) | collective-permute-done | bytes 524320 | tf_op jit(solution)/shard_map/ppermute | solution.py:11
  98.5 2.0 collective-permute-start.5
  100.5 6.2 collective-permute-done.11
  106.8 2.0 collective-permute-start.12
  108.8 1.4 collective-permute-done.5
  110.2 3.8 collective-permute-start.6
  114.1 7.7 %collective-permute-done.12 = bf16[4,256,256]{1,2,0:T(8,128)(2,1)} collective-permute-done((bf16[4,256,256]{1,2,0:T(8,128)(2,1)S(1)}, bf16[4,256,256]{1,2,0:T(8,128)(2,1)}, u32[]{:S(2)}, u32[]{:S(2)}) %collective-permute-start.12) | collective-permute-done | bytes 524320 | tf_op jit(solution)/shard_map/ppermute | solution.py:11
  121.8 1.9 broadcast_select_fusion.15
  123.7 3.9 collective-permute-start.13
  127.6 8.9 %collective-permute-done.6 = bf16[4,256,256]{1,2,0:T(8,128)(2,1)} collective-permute-done((bf16[4,256,256]{1,2,0:T(8,128)(2,1)S(1)}, bf16[4,256,256]{1,2,0:T(8,128)(2,1)}, u32[]{:S(2)}, u32[]{:S(2)}) %collective-permute-start.6) | collective-permute-done | bytes 524320 | tf_op jit(solution)/shard_map/ppermute | solution.py:11
  136.5 1.9 broadcast_select_fusion.31
  138.4 1.6 gather_fusion.1
  141.3 4.9 collective-permute-done.13
  148.3 1.8 convolution_convert_fusion
  150.1 4.3 stack.3
  154.4 6.1 all-to-all-start
  160.5 120.8 %all-gather = s32[128,1,128]{2,1,0:T(1,128)S(1)} all-gather(s32[1,1,128]{2,1,0:T(1,128)S(1)} %bitcast.42), channel_id=1, replica_groups=mesh['row'=16,'col'=8] {'row','col'}, dimensions={0}, use_global_device_ids=true | all-gather | bytes 66048 | tf_op jit(solution)/shard_map/all_gather | solution.py:98
  281.4 74.2 %scatter_custom_fusion = bf16[16384,256]{1,0:T(8,128)(2,1)} fusion(s32[16384]{0:T(1024)S(1)} %compare_select_fusion, bf16[16384,256]{1,0:T(8,128)(2,1)} %bitcast.14, bf16[]{:T(256)} %constant.108.clone.1), kind=kCustom, calls=%fused_computation.8 | custom fusion | bytes 8389120 | tf_op jit(solution)/shard_map/scatter | solution.py:100
  355.6 4.8 convolution_bitcast_fusion
  360.7 29.6 %reduce-scatter.2.cloned.1.call-done = f32[128,256]{0,1:T(8,128)} async-done(((f32[1024,256]{0,1:T(8,128)}), f32[128,256]{0,1:T(8,128)}) %reduce-scatter.2.cloned.1.call-update) | async-done | bytes 131088 | tf_op jit(solution)/shard_map/reduce_scatter | solution.py:104
  390.4 1.5 convert_element_type.41
  392.0 7.7 %fusion.8 = f32[4,256,1024]{2,1,0:T(8,128)} fusion(bf16[4,1024,1024]{2,1,0:T(8,128)(2,1)} %param.11, bf16[4,1024,256]{1,2,0:T(8,128)(2,1)S(1)} %copy.17, bf16[4,256,256]{1,2,0:T(8,128)(2,1)S(1)} %pad_select_fusion.2, bf16[4,256,256]{1,2,0:T(8,128)(2,1)S(1)} %copy-done.4, f32[4,1024]{1,0:T(4,128)S(1)} %add_divide_fusion), kind=kOutput, calls=%fused_computation.59 | convolution fusion | flops 2154823680 | bytes 15745024 | tf_op jit(solution)/shard_map/sij,sjr->sir/dot_general | solution.py:84
  399.8 71.4 %all-gather.3.cloned.1.call-done = bf16[16384,256]{0,1:T(8,128)(2,1)} async-done(((bf16[128,256]{0,1:T(8,128)(2,1)}), bf16[16384,256]{0,1:T(8,128)(2,1)}) %all-gather.3.cloned.1.call-update) | async-done | bytes 8388624 | tf_op jit(solution)/shard_map/all_gather | solution.py:107
  471.2 11.9 %copy.23 = bf16[16384,256]{1,0:T(8,128)(2,1)} copy(bf16[16384,256]{0,1:T(8,128)(2,1)} %all-gather.3.cloned.1.call-done) | data formatting | bytes 16777216 | tf_op jit(solution)/shard_map/all_gather | solution.py:107
  483.1 5.2 gather_fusion
  488.3 3.0 fusion.2
  492.6 1.4 collective-permute-done.14
  494.0 1.6 collective-permute-start.15
  496.4 12.5 %collective-permute-done.15 = bf16[4,256,256]{1,2,0:T(8,128)(2,1)S(1)} collective-permute-done((bf16[4,256,256]{1,2,0:T(8,128)(2,1)S(1)}, bf16[4,256,256]{1,2,0:T(8,128)(2,1)S(1)}, u32[]{:S(2)}, u32[]{:S(2)}) %collective-permute-start.15) | collective-permute-done | bytes 524320 | tf_op jit(solution)/shard_map/ppermute | solution.py:11
  508.9 3.1 collective-permute-start.16
  512.0 8.1 %collective-permute-done.22 = bf16[4,256,256]{1,2,0:T(8,128)(2,1)S(1)} collective-permute-done((bf16[4,256,256]{1,2,0:T(8,128)(2,1)S(1)}, bf16[4,256,256]{1,2,0:T(8,128)(2,1)S(1)}, u32[]{:S(2)}, u32[]{:S(2)}) %collective-permute-start.22) | collective-permute-done | bytes 524320 | tf_op jit(solution)/shard_map/ppermute | solution.py:11
  520.2 3.1 collective-permute-start.23
  523.3 10.3 %collective-permute-done.16 = bf16[4,256,256]{1,2,0:T(8,128)(2,1)S(1)} collective-permute-done((bf16[4,256,256]{1,2,0:T(8,128)(2,1)S(1)}, bf16[4,256,256]{1,2,0:T(8,128)(2,1)S(1)}, u32[]{:S(2)}, u32[]{:S(2)}) %collective-permute-start.16) | collective-permute-done | bytes 524320 | tf_op jit(solution)/shard_map/ppermute | solution.py:11
  534.8 9.3 %collective-permute-done.23 = bf16[4,256,256]{1,2,0:T(8,128)(2,1)S(1)} collective-permute-done((bf16[4,256,256]{1,2,0:T(8,128)(2,1)S(1)}, bf16[4,256,256]{1,2,0:T(8,128)(2,1)S(1)}, u32[]{:S(2)}, u32[]{:S(2)}) %collective-permute-start.23) | collective-permute-done | bytes 524320 | tf_op jit(solution)/shard_map/ppermute | solution.py:11
  546.3 1.8 collective-permute-start.18
  548.2 10.9 %collective-permute-done.24 = bf16[4,256,256]{1,2,0:T(8,128)(2,1)S(1)} collective-permute-done((bf16[4,256,256]{1,2,0:T(8,128)(2,1)S(1)}, bf16[4,256,256]{1,2,0:T(8,128)(2,1)S(1)}, u32[]{:S(2)}, u32[]{:S(2)}) %collective-permute-start.24) | collective-permute-done | bytes 524320 | tf_op jit(solution)/shard_map/ppermute | solution.py:11
  559.2 1.8 collective-permute-start.25
  561.0 10.8 %collective-permute-done.18 = bf16[4,256,256]{1,2,0:T(8,128)(2,1)S(1)} collective-permute-done((bf16[4,256,256]{1,2,0:T(8,128)(2,1)S(1)}, bf16[4,256,256]{1,2,0:T(8,128)(2,1)S(1)}, u32[]{:S(2)}, u32[]{:S(2)}) %collective-permute-start.18) | collective-permute-done | bytes 524320 | tf_op jit(solution)/shard_map/ppermute | solution.py:11
  572.5 9.0 %collective-permute-done.25 = bf16[4,256,256]{1,2,0:T(8,128)(2,1)S(1)} collective-permute-done((bf16[4,256,256]{1,2,0:T(8,128)(2,1)S(1)}, bf16[4,256,256]{1,2,0:T(8,128)(2,1)S(1)}, u32[]{:S(2)}, u32[]{:S(2)}) %collective-permute-start.25) | collective-permute-done | bytes 524320 | tf_op jit(solution)/shard_map/ppermute | solution.py:11
  582.8 2.2 collective-permute-start.20
  585.0 11.4 %collective-permute-done.26 = bf16[4,256,256]{1,2,0:T(8,128)(2,1)S(1)} collective-permute-done((bf16[4,256,256]{1,2,0:T(8,128)(2,1)S(1)}, bf16[4,256,256]{1,2,0:T(8,128)(2,1)S(1)}, u32[]{:S(2)}, u32[]{:S(2)}) %collective-permute-start.26) | collective-permute-done | bytes 524320 | tf_op jit(solution)/shard_map/ppermute | solution.py:11
  597.3 2.2 collective-permute-start.27
  599.5 9.1 %collective-permute-done.20 = bf16[4,256,256]{1,2,0:T(8,128)(2,1)S(1)} collective-permute-done((bf16[4,256,256]{1,2,0:T(8,128)(2,1)S(1)}, bf16[4,256,256]{1,2,0:T(8,128)(2,1)S(1)}, u32[]{:S(2)}, u32[]{:S(2)}) %collective-permute-start.20) | collective-permute-done | bytes 524320 | tf_op jit(solution)/shard_map/ppermute | solution.py:11
  609.6 7.8 %collective-permute-done.27 = bf16[4,256,256]{1,2,0:T(8,128)(2,1)} collective-permute-done((bf16[4,256,256]{1,2,0:T(8,128)(2,1)}, bf16[4,256,256]{1,2,0:T(8,128)(2,1)}, u32[]{:S(2)}, u32[]{:S(2)}) %collective-permute-start.27) | collective-permute-done | bytes 524320 | tf_op jit(solution)/shard_map/ppermute | solution.py:11
  617.4 1.9 broadcast_select_fusion.16
  619.3 1.6 gather_fusion.4
  621.3 1.8 add_convert_fusion
  623.1 3.9 copy.24
  (88 shorter events, 24.5 us)
Async XLA Ops:
  6.5 141.8 %copy-start = (bf16[4,1024,32]{1,2,0:T(8,128)(2,1)S(1)}, bf16[4,1024,32]{1,2,0:T(8,128)(2,1)}, u32[]{:S(2)}) copy-start(bf16[4,1024,32]{1,2,0:T(8,128)(2,1)} %param.12) | copy-start | bytes 786436
  6.5 5.9 copy-start.5
  11.8 3.7 copy-start.3
  11.8 8.8 %copy-start.2 = (bf16[4,256,256]{1,2,0:T(8,128)(2,1)}, bf16[4,256,256]{1,2,0:T(8,128)(2,1)S(1)}, u32[]{:S(2)}) copy-start(bf16[4,256,256]{1,2,0:T(8,128)(2,1)S(1)} %get-tuple-element.15) | copy-start | bytes 1572868
  11.8 3.7 collective-permute-start
  11.9 8.7 %collective-permute-start.7 = (bf16[4,256,256]{1,2,0:T(8,128)(2,1)S(1)}, bf16[4,256,256]{1,2,0:T(8,128)(2,1)}, u32[]{:S(2)}, u32[]{:S(2)}) collective-permute-start(bf16[4,256,256]{1,2,0:T(8,128)(2,1)S(1)} %get-tuple-element.15), channel_id=1, source_target_pairs={{0,1},{1,0},{2,3},{3,2},{4,5},{5,4},{6,7},{7,6},{8,9},{9,8},{10,11... | collective-permute-start | bytes 1572872 | tf_op jit(solution)/shard_map/ppermute | solution.py:11
  16.6 15.0 %collective-permute-start.1 = (bf16[4,256,256]{1,2,0:T(8,128)(2,1)S(1)}, bf16[4,256,256]{1,2,0:T(8,128)(2,1)}, u32[]{:S(2)}, u32[]{:S(2)}) collective-permute-start(bf16[4,256,256]{1,2,0:T(8,128)(2,1)S(1)} %broadcast_select_fusion.19), channel_id=1, source_target_pairs={{0,2},{1,3},{2,0},{3,1},{4,6},{5,7},{6,4},{7,5},{8,10},{9,11},{10,... | collective-permute-start | bytes 1572872 | tf_op jit(solution)/shard_map/ppermute | solution.py:11
  21.7 15.0 %copy-start.1 = (bf16[4,256,256]{1,2,0:T(8,128)(2,1)}, bf16[4,256,256]{1,2,0:T(8,128)(2,1)S(1)}, u32[]{:S(2)}) copy-start(bf16[4,256,256]{1,2,0:T(8,128)(2,1)S(1)} %broadcast_select_fusion.5) | copy-start | bytes 1572868
  21.8 21.1 %collective-permute-start.8 = (bf16[4,256,256]{1,2,0:T(8,128)(2,1)S(1)}, bf16[4,256,256]{1,2,0:T(8,128)(2,1)}, u32[]{:S(2)}, u32[]{:S(2)}) collective-permute-start(bf16[4,256,256]{1,2,0:T(8,128)(2,1)S(1)} %broadcast_select_fusion.5), channel_id=1, source_target_pairs={{0,2},{1,3},{2,0},{3,1},{4,6},{5,7},{6,4},{7,5},{8,10},{9,11},{10,... | collective-permute-start | bytes 1572872 | tf_op jit(solution)/shard_map/ppermute | solution.py:11
  33.5 23.0 %collective-permute-start.2 = (bf16[4,256,256]{1,2,0:T(8,128)(2,1)}, bf16[4,256,256]{1,2,0:T(8,128)(2,1)S(1)}, u32[]{:S(2)}, u32[]{:S(2)}) collective-permute-start(bf16[4,256,256]{1,2,0:T(8,128)(2,1)} %broadcast_select_fusion.21), channel_id=1, source_target_pairs={{0,4},{1,5},{2,6},{3,7},{4,0},{5,1},{6,2},{7,3},{8,12},{9,13},{10,... | collective-permute-start | bytes 1572872 | tf_op jit(solution)/shard_map/ppermute | solution.py:11
  43.9 23.0 %collective-permute-start.9 = (bf16[4,256,256]{1,2,0:T(8,128)(2,1)S(1)}, bf16[4,256,256]{1,2,0:T(8,128)(2,1)}, u32[]{:S(2)}, u32[]{:S(2)}) collective-permute-start(bf16[4,256,256]{1,2,0:T(8,128)(2,1)S(1)} %broadcast_select_fusion.7), channel_id=1, source_target_pairs={{0,4},{1,5},{2,6},{3,7},{4,0},{5,1},{6,2},{7,3},{8,12},{9,13},{10,... | collective-permute-start | bytes 1572872 | tf_op jit(solution)/shard_map/ppermute | solution.py:11
  58.4 14.3 %collective-permute-start.3 = (bf16[4,256,256]{1,2,0:T(8,128)(2,1)}, bf16[4,256,256]{1,2,0:T(8,128)(2,1)}, u32[]{:S(2)}, u32[]{:S(2)}) collective-permute-start(bf16[4,256,256]{1,2,0:T(8,128)(2,1)} %broadcast_select_fusion.23), channel_id=1, source_target_pairs={{0,8},{1,9},{2,10},{3,11},{4,12},{5,13},{6,14},{7,15},{8,0},{9,1},... | collective-permute-start | bytes 1572872 | tf_op jit(solution)/shard_map/ppermute | solution.py:11
  67.0 16.9 %collective-permute-start.10 = (bf16[4,256,256]{1,2,0:T(8,128)(2,1)S(1)}, bf16[4,256,256]{1,2,0:T(8,128)(2,1)}, u32[]{:S(2)}, u32[]{:S(2)}) collective-permute-start(bf16[4,256,256]{1,2,0:T(8,128)(2,1)S(1)} %broadcast_select_fusion.9), channel_id=1, source_target_pairs={{0,8},{1,9},{2,10},{3,11},{4,12},{5,13},{6,14},{7,15},{8,0},{9,1},... | collective-permute-start | bytes 1572872 | tf_op jit(solution)/shard_map/ppermute | solution.py:11
  73.8 23.6 %collective-permute-start.4 = (bf16[4,256,256]{1,2,0:T(8,128)(2,1)S(1)}, bf16[4,256,256]{1,2,0:T(8,128)(2,1)}, u32[]{:S(2)}, u32[]{:S(2)}) collective-permute-start(bf16[4,256,256]{1,2,0:T(8,128)(2,1)S(1)} %broadcast_select_fusion.25), channel_id=1, source_target_pairs={{0,16},{1,17},{2,18},{3,19},{4,20},{5,21},{6,22},{7,23},{8,24},{9,... | collective-permute-start | bytes 1572872 | tf_op jit(solution)/shard_map/ppermute | solution.py:11
  85.0 21.7 %collective-permute-start.11 = (bf16[4,256,256]{1,2,0:T(8,128)(2,1)S(1)}, bf16[4,256,256]{1,2,0:T(8,128)(2,1)S(1)}, u32[]{:S(2)}, u32[]{:S(2)}) collective-permute-start(bf16[4,256,256]{1,2,0:T(8,128)(2,1)S(1)} %broadcast_select_fusion.11), channel_id=1, source_target_pairs={{0,16},{1,17},{2,18},{3,19},{4,20},{5,21},{6,22},{7,23},{8,24},{9,... | collective-permute-start | bytes 1572872 | tf_op jit(solution)/shard_map/ppermute | solution.py:11
  98.5 11.7 %collective-permute-start.5 = (bf16[4,256,256]{1,2,0:T(8,128)(2,1)S(1)}, bf16[4,256,256]{1,2,0:T(8,128)(2,1)S(1)}, u32[]{:S(2)}, u32[]{:S(2)}) collective-permute-start(bf16[4,256,256]{1,2,0:T(8,128)(2,1)S(1)} %broadcast_select_fusion.27), channel_id=1, source_target_pairs={{0,32},{1,33},{2,34},{3,35},{4,36},{5,37},{6,38},{7,39},{8,40},{9,... | collective-permute-start | bytes 1572872 | tf_op jit(solution)/shard_map/ppermute | solution.py:11
  106.8 15.0 %collective-permute-start.12 = (bf16[4,256,256]{1,2,0:T(8,128)(2,1)S(1)}, bf16[4,256,256]{1,2,0:T(8,128)(2,1)}, u32[]{:S(2)}, u32[]{:S(2)}) collective-permute-start(bf16[4,256,256]{1,2,0:T(8,128)(2,1)S(1)} %broadcast_select_fusion.13), channel_id=1, source_target_pairs={{0,32},{1,33},{2,34},{3,35},{4,36},{5,37},{6,38},{7,39},{8,40},{9,... | collective-permute-start | bytes 1572872 | tf_op jit(solution)/shard_map/ppermute | solution.py:11
  110.2 26.3 %collective-permute-start.6 = (bf16[4,256,256]{1,2,0:T(8,128)(2,1)S(1)}, bf16[4,256,256]{1,2,0:T(8,128)(2,1)}, u32[]{:S(2)}, u32[]{:S(2)}) collective-permute-start(bf16[4,256,256]{1,2,0:T(8,128)(2,1)S(1)} %broadcast_select_fusion.29), channel_id=1, source_target_pairs={{0,64},{1,65},{2,66},{3,67},{4,68},{5,69},{6,70},{7,71},{8,72},{9,... | collective-permute-start | bytes 1572872 | tf_op jit(solution)/shard_map/ppermute | solution.py:11
  123.7 22.5 %collective-permute-start.13 = (bf16[4,256,256]{1,2,0:T(8,128)(2,1)}, bf16[4,256,256]{1,2,0:T(8,128)(2,1)}, u32[]{:S(2)}, u32[]{:S(2)}) collective-permute-start(bf16[4,256,256]{1,2,0:T(8,128)(2,1)} %broadcast_select_fusion.15), channel_id=1, source_target_pairs={{0,64},{1,65},{2,66},{3,67},{4,68},{5,69},{6,70},{7,71},{8,72},{9,... | collective-permute-start | bytes 1572872 | tf_op jit(solution)/shard_map/ppermute | solution.py:11
  154.4 6.1 copy-start.6
  154.4 127.0 %all-to-all-start = ((bf16[128,128,256]{2,1,0:T(8,128)(2,1)}), bf16[128,128,256]{2,1,0:T(8,128)(2,1)}, u32[]{:S(2)}, u32[]{:S(2)}) async-start(bf16[128,128,256]{2,1,0:T(8,128)(2,1)} %stack.3), calls=%async_computation | async-start | bytes 16777216 | tf_op jit(solution)/shard_map/all_to_all | solution.py:93
  160.5 229.9 %reduce-scatter.2.cloned.1.call-start = ((), (), s32[]{:S(2)}) async-start(), calls=%async_computation.2 | async-start | bytes 1179648 | tf_op jit(solution)/shard_map/reduce_scatter | solution.py:104
  355.6 36.5 %copy-start.4 = (bf16[4,256,256]{1,2,0:T(8,128)(2,1)S(1)}, bf16[4,256,256]{1,2,0:T(8,128)(2,1)}, u32[]{:S(2)}) copy-start(bf16[4,256,256]{1,2,0:T(8,128)(2,1)} %pad_select_fusion.3) | copy-start | bytes 1572868
  360.4 110.7 %all-gather.3.cloned.1.call-start = ((), (), s32[]{:S(2)}) async-start(), calls=%async_computation.3 | async-start | bytes 8454144 | tf_op jit(solution)/shard_map/all_gather | solution.py:107
  492.0 2.0 collective-permute-start.14
  492.3 3.3 collective-permute-start.21
  494.0 14.8 %collective-permute-start.15 = (bf16[4,256,256]{1,2,0:T(8,128)(2,1)S(1)}, bf16[4,256,256]{1,2,0:T(8,128)(2,1)S(1)}, u32[]{:S(2)}, u32[]{:S(2)}) collective-permute-start(bf16[4,256,256]{1,2,0:T(8,128)(2,1)S(1)} %broadcast_select_fusion.18), channel_id=1, source_target_pairs={{0,2},{1,3},{2,0},{3,1},{4,6},{5,7},{6,4},{7,5},{8,10},{9,11},{10,... | collective-permute-start | bytes 1572872 | tf_op jit(solution)/shard_map/ppermute | solution.py:11
  495.7 24.4 %collective-permute-start.22 = (bf16[4,256,256]{1,2,0:T(8,128)(2,1)S(1)}, bf16[4,256,256]{1,2,0:T(8,128)(2,1)S(1)}, u32[]{:S(2)}, u32[]{:S(2)}) collective-permute-start(bf16[4,256,256]{1,2,0:T(8,128)(2,1)S(1)} %broadcast_select_fusion.4), channel_id=1, source_target_pairs={{0,2},{1,3},{2,0},{3,1},{4,6},{5,7},{6,4},{7,5},{8,10},{9,11},{10,... | collective-permute-start | bytes 1572872 | tf_op jit(solution)/shard_map/ppermute | solution.py:11
  508.9 24.6 %collective-permute-start.16 = (bf16[4,256,256]{1,2,0:T(8,128)(2,1)S(1)}, bf16[4,256,256]{1,2,0:T(8,128)(2,1)S(1)}, u32[]{:S(2)}, u32[]{:S(2)}) collective-permute-start(bf16[4,256,256]{1,2,0:T(8,128)(2,1)S(1)} %broadcast_select_fusion.20), channel_id=1, source_target_pairs={{0,4},{1,5},{2,6},{3,7},{4,0},{5,1},{6,2},{7,3},{8,12},{9,13},{10,... | collective-permute-start | bytes 1572872 | tf_op jit(solution)/shard_map/ppermute | solution.py:11
  520.2 23.9 %collective-permute-start.23 = (bf16[4,256,256]{1,2,0:T(8,128)(2,1)S(1)}, bf16[4,256,256]{1,2,0:T(8,128)(2,1)S(1)}, u32[]{:S(2)}, u32[]{:S(2)}) collective-permute-start(bf16[4,256,256]{1,2,0:T(8,128)(2,1)S(1)} %broadcast_select_fusion.6), channel_id=1, source_target_pairs={{0,4},{1,5},{2,6},{3,7},{4,0},{5,1},{6,2},{7,3},{8,12},{9,13},{10,... | collective-permute-start | bytes 1572872 | tf_op jit(solution)/shard_map/ppermute | solution.py:11
  533.6 12.7 %collective-permute-start.17 = (bf16[4,256,256]{1,2,0:T(8,128)(2,1)S(1)}, bf16[4,256,256]{1,2,0:T(8,128)(2,1)S(1)}, u32[]{:S(2)}, u32[]{:S(2)}) collective-permute-start(bf16[4,256,256]{1,2,0:T(8,128)(2,1)S(1)} %broadcast_select_fusion.22), channel_id=1, source_target_pairs={{0,8},{1,9},{2,10},{3,11},{4,12},{5,13},{6,14},{7,15},{8,0},{9,1},... | collective-permute-start | bytes 1572872 | tf_op jit(solution)/shard_map/ppermute | solution.py:11
  544.2 14.9 %collective-permute-start.24 = (bf16[4,256,256]{1,2,0:T(8,128)(2,1)S(1)}, bf16[4,256,256]{1,2,0:T(8,128)(2,1)S(1)}, u32[]{:S(2)}, u32[]{:S(2)}) collective-permute-start(bf16[4,256,256]{1,2,0:T(8,128)(2,1)S(1)} %broadcast_select_fusion.8), channel_id=1, source_target_pairs={{0,8},{1,9},{2,10},{3,11},{4,12},{5,13},{6,14},{7,15},{8,0},{9,1},... | collective-permute-start | bytes 1572872 | tf_op jit(solution)/shard_map/ppermute | solution.py:11
  546.3 25.5 %collective-permute-start.18 = (bf16[4,256,256]{1,2,0:T(8,128)(2,1)S(1)}, bf16[4,256,256]{1,2,0:T(8,128)(2,1)S(1)}, u32[]{:S(2)}, u32[]{:S(2)}) collective-permute-start(bf16[4,256,256]{1,2,0:T(8,128)(2,1)S(1)} %broadcast_select_fusion.24), channel_id=1, source_target_pairs={{0,16},{1,17},{2,18},{3,19},{4,20},{5,21},{6,22},{7,23},{8,24},{9,... | collective-permute-start | bytes 1572872 | tf_op jit(solution)/shard_map/ppermute | solution.py:11
  559.2 22.3 %collective-permute-start.25 = (bf16[4,256,256]{1,2,0:T(8,128)(2,1)S(1)}, bf16[4,256,256]{1,2,0:T(8,128)(2,1)S(1)}, u32[]{:S(2)}, u32[]{:S(2)}) collective-permute-start(bf16[4,256,256]{1,2,0:T(8,128)(2,1)S(1)} %broadcast_select_fusion.10), channel_id=1, source_target_pairs={{0,16},{1,17},{2,18},{3,19},{4,20},{5,21},{6,22},{7,23},{8,24},{9,... | collective-permute-start | bytes 1572872 | tf_op jit(solution)/shard_map/ppermute | solution.py:11
  571.9 10.8 %collective-permute-start.19 = (bf16[4,256,256]{1,2,0:T(8,128)(2,1)S(1)}, bf16[4,256,256]{1,2,0:T(8,128)(2,1)S(1)}, u32[]{:S(2)}, u32[]{:S(2)}) collective-permute-start(bf16[4,256,256]{1,2,0:T(8,128)(2,1)S(1)} %broadcast_select_fusion.26), channel_id=1, source_target_pairs={{0,32},{1,33},{2,34},{3,35},{4,36},{5,37},{6,38},{7,39},{8,40},{9,... | collective-permute-start | bytes 1572872 | tf_op jit(solution)/shard_map/ppermute | solution.py:11
  581.5 14.9 %collective-permute-start.26 = (bf16[4,256,256]{1,2,0:T(8,128)(2,1)S(1)}, bf16[4,256,256]{1,2,0:T(8,128)(2,1)S(1)}, u32[]{:S(2)}, u32[]{:S(2)}) collective-permute-start(bf16[4,256,256]{1,2,0:T(8,128)(2,1)S(1)} %broadcast_select_fusion.12), channel_id=1, source_target_pairs={{0,32},{1,33},{2,34},{3,35},{4,36},{5,37},{6,38},{7,39},{8,40},{9,... | collective-permute-start | bytes 1572872 | tf_op jit(solution)/shard_map/ppermute | solution.py:11
  582.8 25.8 %collective-permute-start.20 = (bf16[4,256,256]{1,2,0:T(8,128)(2,1)S(1)}, bf16[4,256,256]{1,2,0:T(8,128)(2,1)S(1)}, u32[]{:S(2)}, u32[]{:S(2)}) collective-permute-start(bf16[4,256,256]{1,2,0:T(8,128)(2,1)S(1)} %broadcast_select_fusion.28), channel_id=1, source_target_pairs={{0,64},{1,65},{2,66},{3,67},{4,68},{5,69},{6,70},{7,71},{8,72},{9,... | collective-permute-start | bytes 1572872 | tf_op jit(solution)/shard_map/ppermute | solution.py:11
  597.3 20.1 %collective-permute-start.27 = (bf16[4,256,256]{1,2,0:T(8,128)(2,1)}, bf16[4,256,256]{1,2,0:T(8,128)(2,1)}, u32[]{:S(2)}, u32[]{:S(2)}) collective-permute-start(bf16[4,256,256]{1,2,0:T(8,128)(2,1)} %broadcast_select_fusion.14), channel_id=1, source_target_pairs={{0,64},{1,65},{2,66},{3,67},{4,68},{5,69},{6,70},{7,71},{8,72},{9,... | collective-permute-start | bytes 1572872 | tf_op jit(solution)/shard_map/ppermute | solution.py:11
Sparse Core Ops, SparseCore 0:
  360.6 29.7 reduce-scatter.1
  393.2 77.9 all-gather.2
